TPU v7x, 128 devices: a whole 4x4x4 slice. The times are simulated.
128 devices in a mesh: row: 16 (over y_hi, z, core), col: 8 (over x, y_lo).
Axes of the slice: x: 4, y: 4 (y_hi: 2, y_lo: 2; y = y_hi * 2 + y_lo), z: 4, core: 2. Of those that a mesh axis runs over, the one named last changes fastest.
Arguments:
- factor: bfloat16 [16, 1536, 6144], P(None, 'row'), may hold values from -0.078125 to 0.078125
- inverse_blocks: bfloat16 [4, 1536, 1536], P(None, 'row'), as said below
- right_side: float32 [16, 1536, 4096], P(None, 'row', 'col'), may hold values from -6 to 6
- shape_derivative: float32 [4, 1536, 4096], P(None, 'row', 'col')
Outputs:
- solved: float32 [4, 1536, 4096], P(None, 'row', 'col')
- trailing: float32 [12, 1536, 4096], P(None, 'row', 'col')
- sensitivity: float32 [4, 1536], P(None, 'row')
Inputs may be any that keep to these rules, and one draw needn't show every extreme that they name: inverse_blocks[k] is the inverse supplied for the diagonal block of step k.
All inputs are finite; a program needn't handle non-finite values.
Results may differ from a plain program's by a relative error of at most 0.0045.
Values may be sent and summed in bfloat16 or wider, within the bound.
No kernel may reach another device: no remote copies, remote signals or barrier semaphores. Data moves between devices by JAX's collectives and lax.ppermute only.
A program may use at most 128 MiB of HBM per device.

v0:
```python
import jax
import jax.numpy as jnp
from jax import lax
from jax.sharding import PartitionSpec as P


def local(factor, inverse_blocks, right_side, shape_derivative):
    step_count = inverse_blocks.shape[0]
    block_size = inverse_blocks.shape[2]
    solved_list = []
    accum = right_side
    for step in range(step_count):
        residual = accum[step]
        gathered = lax.all_gather(residual.astype(jnp.bfloat16), "row", axis=0, tiled=True)
        own_rows = jnp.dot(inverse_blocks[step], gathered, preferred_element_type=jnp.float32)
        spread = lax.all_gather(own_rows.astype(jnp.bfloat16), "row", axis=0, tiled=True)
        own_rows, spread = (own_rows, spread)
        solved_list.append(own_rows)
        lower = factor[step + 1 :, :, step * block_size : (step + 1) * block_size]
        update = jnp.einsum("bij,jq->biq", lower, spread, preferred_element_type=jnp.float32)
        accum = jnp.concatenate([accum[: step + 1], accum[step + 1 :] - update], axis=0)
    trailing = accum[step_count:]
    solved = jnp.stack(solved_list)
    partial_terms = jnp.sum(solved * shape_derivative, axis=2)
    sensitivity = lax.psum(partial_terms, "col")
    return (solved, trailing, sensitivity)


def solution(mesh):
    placed = (
        P(None, "row", None),
        P(None, "row", None),
        P(None, "row", "col"),
        P(None, "row", "col"),
    )
    return jax.shard_map(
        local,
        mesh=mesh,
        in_specs=placed,
        out_specs=(P(None, "row", "col"), P(None, "row", "col"), P(None, "row")),
        check_vma=False,
    )
```

profile of v0, /device:TPU:1, one launch (start us, length us, event | category | flops | bytes accessed | tf_op | source)
XLA Modules:
  0.0 424.7 jit_solution(16260220490646862225)
XLA Ops:
  7.2 1.6 slice.118
  8.8 0.0 all-gather.13.cloned.1.call-start
  8.9 51.9 %all-gather.21.cloned.1.call-done = bf16[1,1536,512]{2,1,0:T(8,128)(2,1)} async-done(((bf16[1,96,512]{2,1,0:T(8,128)(2,1)}), bf16[1,1536,512]{2,1,0:T(8,128)(2,1)}) %all-gather.21.cloned.1.call-update) | async-done | bytes 1572880 | tf_op jit(solution)/shard_map/all_gather | solution.py:14
  60.7 2.5 fusion.36
  63.3 0.0 all-gather.23.cloned.1.call-start
  63.4 45.3 %all-gather.13.cloned.1.call-done = bf16[1536,512]{1,0:T(8,128)(2,1)} async-done(((bf16[96,512]{1,0:T(8,128)(2,1)}), bf16[1536,512]{1,0:T(8,128)(2,1)}) %all-gather.13.cloned.1.call-update) | async-done | bytes 1572880 | tf_op jit(solution)/shard_map/all_gather | solution.py:16
  108.6 6.3 %bitcast_subtract_fusion = f32[15,96,512]{2,1,0:T(8,128)S(1)} fusion(f32[16,96,512]{2,1,0:T(8,128)} %param.6, bf16[16,96,6144]{2,1,0:T(8,128)(2,1)} %param.4, bf16[1536,512]{1,0:T(8,128)(2,1)} %all-gather.13.cloned.1.call-done), kind=kOutput, calls=%fused_computation.8 | convolution fusion | flops 2265661440 | bytes 11894784 | tf_op jit(solution)/shard_map/bij,jq->biq/dot_general | solution.py:20
  114.9 1.6 copy-done.4
  116.5 0.7 slice.117
  117.2 0.0 all-gather.15.cloned.1.call-start
  117.2 44.9 %all-gather.23.cloned.1.call-done = bf16[1,1536,512]{2,1,0:T(8,128)(2,1)} async-done(((bf16[1,96,512]{2,1,0:T(8,128)(2,1)}), bf16[1,1536,512]{2,1,0:T(8,128)(2,1)}) %all-gather.23.cloned.1.call-update) | async-done | bytes 1572880 | tf_op jit(solution)/shard_map/all_gather | solution.py:14
  162.1 2.4 bitcast_convert_fusion.2
  164.6 0.0 all-gather.25.cloned.1.call-start
  164.6 45.2 %all-gather.15.cloned.1.call-done = bf16[1536,512]{1,0:T(8,128)(2,1)} async-done(((bf16[96,512]{1,0:T(8,128)(2,1)}), bf16[1536,512]{1,0:T(8,128)(2,1)}) %all-gather.15.cloned.1.call-update) | async-done | bytes 1572880 | tf_op jit(solution)/shard_map/all_gather | solution.py:16
  209.9 5.9 %slice_subtract_fusion = f32[14,96,512]{2,1,0:T(8,128)S(1)} fusion(f32[15,96,512]{2,1,0:T(8,128)} %copy-done.4, bf16[16,96,6144]{2,1,0:T(8,128)(2,1)} %param.4, bf16[1536,512]{1,0:T(8,128)(2,1)} %all-gather.15.cloned.1.call-done), kind=kOutput, calls=%fused_computation.9 | convolution fusion | flops 2114617344 | bytes 11206656 | tf_op jit(solution)/shard_map/bij,jq->biq/dot_general | solution.py:20
  215.8 1.5 copy-done.3
  217.3 0.7 slice.116
  218.0 0.0 all-gather.17.cloned.1.call-start
  218.1 44.9 %all-gather.25.cloned.1.call-done = bf16[1,1536,512]{2,1,0:T(8,128)(2,1)} async-done(((bf16[1,96,512]{2,1,0:T(8,128)(2,1)}), bf16[1,1536,512]{2,1,0:T(8,128)(2,1)}) %all-gather.25.cloned.1.call-update) | async-done | bytes 1572880 | tf_op jit(solution)/shard_map/all_gather | solution.py:14
  263.0 2.4 bitcast_convert_fusion.1
  265.4 0.0 all-gather.27.cloned.1.call-start
  265.5 45.2 %all-gather.17.cloned.1.call-done = bf16[1536,512]{1,0:T(8,128)(2,1)} async-done(((bf16[96,512]{1,0:T(8,128)(2,1)}), bf16[1536,512]{1,0:T(8,128)(2,1)}) %all-gather.17.cloned.1.call-update) | async-done | bytes 1572880 | tf_op jit(solution)/shard_map/all_gather | solution.py:16
  310.7 5.5 %slice_subtract_fusion.1 = f32[13,96,512]{2,1,0:T(8,128)S(1)} fusion(f32[14,96,512]{2,1,0:T(8,128)} %copy-done.3, bf16[16,96,6144]{2,1,0:T(8,128)(2,1)} %param.4, bf16[1536,512]{1,0:T(8,128)(2,1)} %all-gather.17.cloned.1.call-done), kind=kOutput, calls=%fused_computation.10 | convolution fusion | flops 1963573248 | bytes 10518528 | tf_op jit(solution)/shard_map/bij,jq->biq/dot_general | solution.py:20
  316.2 1.5 copy-done.2
  317.7 0.7 slice.115
  318.4 0.0 all-gather.19.cloned.1.call-start
  318.4 44.9 %all-gather.27.cloned.1.call-done = bf16[1,1536,512]{2,1,0:T(8,128)(2,1)} async-done(((bf16[1,96,512]{2,1,0:T(8,128)(2,1)}), bf16[1,1536,512]{2,1,0:T(8,128)(2,1)}) %all-gather.27.cloned.1.call-update) | async-done | bytes 1572880 | tf_op jit(solution)/shard_map/all_gather | solution.py:14
  363.3 2.4 bitcast_convert_fusion
  365.8 1.0 multiply_reduce_fusion
  366.8 15.6 %psum.7 = f32[4,96]{1,0:T(4,128)} all-reduce(f32[4,96]{1,0:T(4,128)S(1)} %get-tuple-element.3), channel_id=1, replica_groups=mesh['row'=16,'col'=8] {'col'}, use_global_device_ids=true, to_apply=%region_1.0 | all-reduce | flops 384 | bytes 3072 | tf_op jit(solution)/shard_map/psum | solution.py:25
  382.3 28.9 %all-gather.19.cloned.1.call-done = bf16[1536,512]{1,0:T(8,128)(2,1)} async-done(((bf16[96,512]{1,0:T(8,128)(2,1)}), bf16[1536,512]{1,0:T(8,128)(2,1)}) %all-gather.19.cloned.1.call-update) | async-done | bytes 1572880 | tf_op jit(solution)/shard_map/all_gather | solution.py:16
  411.2 6.6 %slice_subtract_fusion.2 = f32[12,96,512]{2,1,0:T(8,128)} fusion(f32[13,96,512]{2,1,0:T(8,128)} %copy-done.2, bf16[16,96,6144]{2,1,0:T(8,128)(2,1)} %param.4, bf16[1536,512]{1,0:T(8,128)(2,1)} %all-gather.19.cloned.1.call-done), kind=kOutput, calls=%fused_computation.11 | convolution fusion | flops 1812529152 | bytes 9830400 | tf_op jit(solution)/shard_map/bij,jq->biq/dot_general | solution.py:20
  (16 shorter events, 0.2 us)
Async XLA Ops:
  7.2 53.6 %all-gather.21.cloned.1.call-start = ((), (), s32[]{:S(2)}) async-start(), calls=%async_computation.4 | async-start | bytes 1671168 | tf_op jit(solution)/shard_map/all_gather | solution.py:14
  8.8 99.8 %all-gather.13.cloned.1.call-start = ((), (), s32[]{:S(2)}) async-start(), calls=%async_computation | async-start | bytes 1671168 | tf_op jit(solution)/shard_map/all_gather | solution.py:16
  63.3 98.8 %copy-start = (bf16[4,96,1536]{2,1,0:T(8,128)(2,1)S(1)}, bf16[4,96,1536]{2,1,0:T(8,128)(2,1)}, u32[]{:S(2)}) copy-start(bf16[4,96,1536]{2,1,0:T(8,128)(2,1)} %param.5) | copy-start | bytes 3538948
  63.3 98.8 %all-gather.23.cloned.1.call-start = ((), (), s32[]{:S(2)}) async-start(), calls=%async_computation.5 | async-start | bytes 1671168 | tf_op jit(solution)/shard_map/all_gather | solution.py:14
  114.9 1.6 copy-start.4
  117.2 92.7 %all-gather.15.cloned.1.call-start = ((), (), s32[]{:S(2)}) async-start(), calls=%async_computation.1 | async-start | bytes 1671168 | tf_op jit(solution)/shard_map/all_gather | solution.py:16
  164.6 98.4 %all-gather.25.cloned.1.call-start = ((), (), s32[]{:S(2)}) async-start(), calls=%async_computation.6 | async-start | bytes 1671168 | tf_op jit(solution)/shard_map/all_gather | solution.py:14
  215.8 1.5 copy-start.3
  218.0 92.7 %all-gather.17.cloned.1.call-start = ((), (), s32[]{:S(2)}) async-start(), calls=%async_computation.2 | async-start | bytes 1671168 | tf_op jit(solution)/shard_map/all_gather | solution.py:16
  265.4 97.9 %all-gather.27.cloned.1.call-start = ((), (), s32[]{:S(2)}) async-start(), calls=%async_computation.7 | async-start | bytes 1671168 | tf_op jit(solution)/shard_map/all_gather | solution.py:14
  316.2 1.5 copy-start.2
  317.7 48.1 %copy-start.1 = (f32[4,96,512]{2,1,0:T(8,128)S(1)}, f32[4,96,512]{2,1,0:T(8,128)}, u32[]{:S(2)}) copy-start(f32[4,96,512]{2,1,0:T(8,128)} %param.7) | copy-start | bytes 2359300
  318.4 92.8 %all-gather.19.cloned.1.call-start = ((), (), s32[]{:S(2)}) async-start(), calls=%async_computation.3 | async-start | bytes 1671168 | tf_op jit(solution)/shard_map/all_gather | solution.py:16
Sparse Core Ops, SparseCore 0:
  11.0 49.6 all-gather.20
  63.8 44.7 all-gather.12
  117.3 44.7 all-gather.22
  165.0 44.7 all-gather.14
  218.1 44.7 all-gather.24
  265.9 44.7 all-gather.16
  318.5 44.7 all-gather.26
  366.4 44.7 all-gather.18
where the time goes:
time: 425 us
  waiting for transfers between devices  351 us (83%)
  matrix products  34.2 us (8%)
  blocking collectives  15.6 us (4%)
  between operations  14.2 us (3%)
  local copies, waits for them, and re-layouts  8.14 us (2%)
    all_gather x4, waiting for transfers between devices, local(): lax.all_gather(residual.astype(jnp.bfloat16), 'row', axis=0, tiled=True)  187 us
    all_gather x4, waiting for transfers between devices, local(): lax.all_gather(own_rows.astype(jnp.bfloat16), 'row', axis=0, tiled=True)  165 us
    dot_general x4, matrix products, local(): jnp.einsum('bij,jq->biq', lower, spread, preferred_element_type=jnp.float32)  24.3 us
    psum x1, blocking collectives, local(): sensitivity = lax.psum(partial_terms, 'col')  15.6 us
    dot_general x4, matrix products, local(): jnp.dot(inverse_blocks[step], gathered, preferred_element_type=jnp.float32)  9.85 us
  transfers between devices with their start and end apart: 8, of which 8 were waited for; matrix products, arithmetic and copies ran while one was open for 0% of the time, Pallas kernels for 0%

commit v1 on v0

--- a/solution.py
+++ b/solution.py
@@ -11,7 +11,11 @@
     accum = right_side
     for step in range(step_count):
         residual = accum[step]
-        gathered = lax.all_gather(residual.astype(jnp.bfloat16), "row", axis=0, tiled=True)
+        block = residual.astype(jnp.bfloat16)
+        peers = lax.axis_size("row")
+        pieces = jnp.stack([block for _ in range(peers)])
+        pieces = lax.all_to_all(pieces, "row", split_axis=0, concat_axis=0)
+        gathered = jnp.concatenate(pieces, axis=0)
         own_rows = jnp.dot(inverse_blocks[step], gathered, preferred_element_type=jnp.float32)
         spread = lax.all_gather(own_rows.astype(jnp.bfloat16), "row", axis=0, tiled=True)
         own_rows, spread = (own_rows, spread)

time: 425 us -> 334 us (0.79)
  waiting for transfers between devices: 351 us -> 161 us
  blocking collectives: 15.6 us -> 127 us
  local copies, waits for them, and re-layouts: 8.14 us -> 1.66 us
  matrix products: 34.2 us -> 28.5 us
    all_gather x4 -> x0, waiting for transfers between devices: 187 us -> none  [local(): lax.all_gather(residual.astype(jnp.bfloat16), 'row', axis=0, tiled=True)]
    all_to_all x0 -> x4, blocking collectives: none -> 111 us  [local(): pieces = lax.all_to_all(pieces, 'row', split_axis=0, concat_axis=0)]
    dot_general x4, matrix products: 9.85 us -> 4.13 us  [local(): jnp.dot(inverse_blocks[step], gathered, preferred_element_type=jnp.float32)]
    unnamed x10, local copies, waits for them, and re-layouts: 4.6 us -> 0.09 us
  transfers between devices with their start and end apart: 8 -> 4, of which waited for: 8 -> 4; matrix products, arithmetic and copies ran while one was open for 0% -> 0% of each run, Pallas kernels for 0% -> 0%
where the time goes in v1:
time: 334 us; the launch traced here: 333 us
  waiting for transfers between devices  161 us (48%)
  blocking collectives  127 us (38%)
  matrix products  28.5 us (9%)
  between operations  13.9 us (4%)
    all_gather x4, waiting for transfers between devices, local(): lax.all_gather(own_rows.astype(jnp.bfloat16), 'row', axis=0, tiled=True)  161 us
    all_to_all x4, blocking collectives, local(): pieces = lax.all_to_all(pieces, 'row', split_axis=0, concat_axis=0)  111 us
    dot_general x4, matrix products, local(): jnp.einsum('bij,jq->biq', lower, spread, preferred_element_type=jnp.float32)  24.3 us
    psum x1, blocking collectives, local(): sensitivity = lax.psum(partial_terms, 'col')  16.3 us
  transfers between devices with their start and end apart: 4, of which 4 were waited for; matrix products, arithmetic and copies ran while one was open for 0% of the time, Pallas kernels for 0%

profile of v1, /device:TPU:1, one launch (start us, length us, event | category | flops | bytes accessed | tf_op | source)
XLA Modules:
  0.0 333.5 jit_solution(2946057854177174953)
XLA Ops:
  7.2 0.0 all-gather.5.cloned.1.call-start
  7.2 0.9 fusion.32
  8.2 0.1 stack.27
  8.3 31.8 %all_to_all.20 = bf16[16,96,512]{2,1,0:T(8,128)(2,1)S(1)} all-to-all(bf16[16,96,512]{2,1,0:T(8,128)(2,1)S(1)} %stack.27), channel_id=1, replica_groups=mesh['row'=16,'col'=8] {'row'}, dimensions={0} | all-to-all | bytes 3145728 | tf_op jit(solution)/shard_map/all_to_all | solution.py:17
  40.1 1.0 fusion.36
  41.1 0.0 all-gather.5.cloned.1.call-update
  41.2 0.0 all-gather.7.cloned.1.call-start
  41.2 44.3 %all-gather.5.cloned.1.call-done = bf16[1536,512]{1,0:T(8,128)(2,1)} async-done(((bf16[96,512]{1,0:T(8,128)(2,1)}), bf16[1536,512]{1,0:T(8,128)(2,1)}) %all-gather.5.cloned.1.call-update) | async-done | bytes 1572880 | tf_op jit(solution)/shard_map/all_gather | solution.py:20
  85.5 6.3 %bitcast_subtract_fusion = f32[15,96,512]{2,1,0:T(8,128)S(1)} fusion(f32[16,96,512]{2,1,0:T(8,128)} %param.6, bf16[16,96,6144]{2,1,0:T(8,128)(2,1)} %param.4, bf16[1536,512]{1,0:T(8,128)(2,1)} %all-gather.5.cloned.1.call-done), kind=kOutput, calls=%fused_computation.8 | convolution fusion | flops 2265661440 | bytes 11894784 | tf_op jit(solution)/shard_map/bij,jq->biq/dot_general | solution.py:24
  91.8 0.1 stack.30
  92.0 26.3 %all_to_all.21 = bf16[16,96,512]{2,1,0:T(8,128)(2,1)S(1)} all-to-all(bf16[16,96,512]{2,1,0:T(8,128)(2,1)S(1)} %stack.30), channel_id=1, replica_groups=mesh['row'=16,'col'=8] {'row'}, dimensions={0} | all-to-all | bytes 3145728 | tf_op jit(solution)/shard_map/all_to_all | solution.py:17
  118.3 1.0 bitcast_convert_fusion.2
  119.3 0.0 all-gather.7.cloned.1.call-update
  119.3 0.0 all-gather.9.cloned.1.call-start
  119.4 44.7 %all-gather.7.cloned.1.call-done = bf16[1536,512]{1,0:T(8,128)(2,1)} async-done(((bf16[96,512]{1,0:T(8,128)(2,1)}), bf16[1536,512]{1,0:T(8,128)(2,1)}) %all-gather.7.cloned.1.call-update) | async-done | bytes 1572880 | tf_op jit(solution)/shard_map/all_gather | solution.py:20
  164.1 5.9 %slice_subtract_fusion = f32[14,96,512]{2,1,0:T(8,128)S(1)} fusion(f32[15,96,512]{2,1,0:T(8,128)} %copy-done.4, bf16[16,96,6144]{2,1,0:T(8,128)(2,1)} %param.4, bf16[1536,512]{1,0:T(8,128)(2,1)} %all-gather.7.cloned.1.call-done), kind=kOutput, calls=%fused_computation.9 | convolution fusion | flops 2114617344 | bytes 11206656 | tf_op jit(solution)/shard_map/bij,jq->biq/dot_general | solution.py:24
  170.1 0.1 stack.33
  170.3 26.3 %all_to_all.22 = bf16[16,96,512]{2,1,0:T(8,128)(2,1)S(1)} all-to-all(bf16[16,96,512]{2,1,0:T(8,128)(2,1)S(1)} %stack.33), channel_id=1, replica_groups=mesh['row'=16,'col'=8] {'row'}, dimensions={0} | all-to-all | bytes 3145728 | tf_op jit(solution)/shard_map/all_to_all | solution.py:17
  196.6 1.0 bitcast_convert_fusion.1
  197.6 0.0 all-gather.9.cloned.1.call-update
  197.6 0.0 all-gather.11.cloned.1.call-start
  197.7 44.7 %all-gather.9.cloned.1.call-done = bf16[1536,512]{1,0:T(8,128)(2,1)} async-done(((bf16[96,512]{1,0:T(8,128)(2,1)}), bf16[1536,512]{1,0:T(8,128)(2,1)}) %all-gather.9.cloned.1.call-update) | async-done | bytes 1572880 | tf_op jit(solution)/shard_map/all_gather | solution.py:20
  242.4 5.5 %slice_subtract_fusion.1 = f32[13,96,512]{2,1,0:T(8,128)S(1)} fusion(f32[14,96,512]{2,1,0:T(8,128)} %copy-done.3, bf16[16,96,6144]{2,1,0:T(8,128)(2,1)} %param.4, bf16[1536,512]{1,0:T(8,128)(2,1)} %all-gather.9.cloned.1.call-done), kind=kOutput, calls=%fused_computation.10 | convolution fusion | flops 1963573248 | bytes 10518528 | tf_op jit(solution)/shard_map/bij,jq->biq/dot_general | solution.py:24
  248.0 0.1 stack.36
  248.1 26.3 %all_to_all.23 = bf16[16,96,512]{2,1,0:T(8,128)(2,1)S(1)} all-to-all(bf16[16,96,512]{2,1,0:T(8,128)(2,1)S(1)} %stack.36), channel_id=1, replica_groups=mesh['row'=16,'col'=8] {'row'}, dimensions={0} | all-to-all | bytes 3145728 | tf_op jit(solution)/shard_map/all_to_all | solution.py:17
  274.4 1.0 bitcast_convert_fusion
  275.5 0.0 all-gather.11.cloned.1.call-update
  275.5 0.1 copy-done.1
  275.6 1.0 multiply_reduce_fusion
  276.5 16.3 %psum.7 = f32[4,96]{1,0:T(4,128)} all-reduce(f32[4,96]{1,0:T(4,128)S(1)} %get-tuple-element.3), channel_id=1, replica_groups=mesh['row'=16,'col'=8] {'col'}, use_global_device_ids=true, to_apply=%region_1.0 | all-reduce | flops 384 | bytes 3072 | tf_op jit(solution)/shard_map/psum | solution.py:29
  292.9 27.5 %all-gather.11.cloned.1.call-done = bf16[1536,512]{1,0:T(8,128)(2,1)} async-done(((bf16[96,512]{1,0:T(8,128)(2,1)}), bf16[1536,512]{1,0:T(8,128)(2,1)}) %all-gather.11.cloned.1.call-update) | async-done | bytes 1572880 | tf_op jit(solution)/shard_map/all_gather | solution.py:20
  320.3 6.6 %slice_subtract_fusion.2 = f32[12,96,512]{2,1,0:T(8,128)} fusion(f32[13,96,512]{2,1,0:T(8,128)} %copy-done.2, bf16[16,96,6144]{2,1,0:T(8,128)(2,1)} %param.4, bf16[1536,512]{1,0:T(8,128)(2,1)} %all-gather.11.cloned.1.call-done), kind=kOutput, calls=%fused_computation.11 | convolution fusion | flops 1812529152 | bytes 9830400 | tf_op jit(solution)/shard_map/bij,jq->biq/dot_general | solution.py:24
  (12 shorter events, 0.1 us)
Async XLA Ops:
  7.2 78.3 %all-gather.5.cloned.1.call-start = ((), (), s32[]{:S(2)}) async-start(), calls=%async_computation.4 | async-start | bytes 1671168 | tf_op jit(solution)/shard_map/all_gather | solution.py:20
  8.3 31.8 %copy-start = (bf16[4,96,1536]{2,1,0:T(8,128)(2,1)S(1)}, bf16[4,96,1536]{2,1,0:T(8,128)(2,1)}, u32[]{:S(2)}) copy-start(bf16[4,96,1536]{2,1,0:T(8,128)(2,1)} %param.5) | copy-start | bytes 3538948
  41.2 123.0 %all-gather.7.cloned.1.call-start = ((), (), s32[]{:S(2)}) async-start(), calls=%async_computation.5 | async-start | bytes 1671168 | tf_op jit(solution)/shard_map/all_gather | solution.py:20
  91.8 26.5 %copy-start.4 = (f32[15,96,512]{2,1,0:T(8,128)}, f32[15,96,512]{2,1,0:T(8,128)S(1)}, u32[]{:S(2)}) copy-start(f32[15,96,512]{2,1,0:T(8,128)S(1)} %bitcast_subtract_fusion) | copy-start | bytes 8847364
  119.3 123.1 %all-gather.9.cloned.1.call-start = ((), (), s32[]{:S(2)}) async-start(), calls=%async_computation.6 | async-start | bytes 1671168 | tf_op jit(solution)/shard_map/all_gather | solution.py:20
  170.1 26.5 %copy-start.3 = (f32[14,96,512]{2,1,0:T(8,128)}, f32[14,96,512]{2,1,0:T(8,128)S(1)}, u32[]{:S(2)}) copy-start(f32[14,96,512]{2,1,0:T(8,128)S(1)} %slice_subtract_fusion) | copy-start | bytes 8257540
  197.6 122.7 %all-gather.11.cloned.1.call-start = ((), (), s32[]{:S(2)}) async-start(), calls=%async_computation.7 | async-start | bytes 1671168 | tf_op jit(solution)/shard_map/all_gather | solution.py:20
  247.9 26.5 %copy-start.2 = (f32[13,96,512]{2,1,0:T(8,128)}, f32[13,96,512]{2,1,0:T(8,128)S(1)}, u32[]{:S(2)}) copy-start(f32[13,96,512]{2,1,0:T(8,128)S(1)} %slice_subtract_fusion.1) | copy-start | bytes 7667716
  274.4 1.1 copy-start.1
Sparse Core Ops, SparseCore 0:
  41.3 44.1 all-gather.4
  119.4 44.6 all-gather.6
  197.7 44.6 all-gather.8
  275.6 44.6 all-gather.10
